TPU v7x, 32 devices: a whole 2x2x4 slice. The times are simulated.
32 devices in a mesh: seq: 8 (over z, x), chan: 4 (over y, core).
Axes of the slice: x: 2, y: 2, z: 4, core: 2. Of those that a mesh axis runs over, the one named last changes fastest.
Arguments:
- signal: float32 [256, 65536], P('chan', 'seq'), may hold values from -6 to 6
- gating: float32 [256, 65536], P('chan', 'seq'), may hold values from -6 to 6
- response: float32 [256, 65536], P('chan', 'seq'), may hold values from -0.0234375 to 0.0234375
- skip_gain: float32 [256], P('chan'), may hold values from -4 to 4
- mixing_weight: float32 [256, 256], P(None, 'chan'), may hold values from -0.5 to 0.5
Outputs:
- output: float32 [256, 65536], P('chan', 'seq')
All inputs are finite; a program needn't handle non-finite values.
Results may differ from a plain program's by a relative error of at most 0.00007.
Values sent between devices are 32-bit elements; how exact they have to be, the bound alone decides.
A program may use at most 128 MiB of HBM per device.

v0:
```python
from functools import partial
import math
import jax
import jax.numpy as jnp
import numpy as np
from jax import lax
from jax.sharding import PartitionSpec as P


def twiddle(number, period):
    angle = (number % period).astype(jnp.float32) * (2.0 * math.pi / period)
    return (jnp.cos(angle), jnp.sin(angle))


def rotate(real_part, imag_part, cos_part, sin_part):
    return (
        real_part * cos_part - imag_part * sin_part,
        imag_part * cos_part + real_part * sin_part,
    )


def dft_table(length, sign):
    steps = jnp.arange(length, dtype=jnp.int32)
    cos_part, sin_part = twiddle(steps[:, None] * steps[None, :], length)
    return (cos_part, sign * sin_part)


def complex_apply(pattern, table_real, table_imag, real_part, imag_part):
    contract = partial(jnp.einsum, pattern, precision=lax.Precision.HIGHEST)
    return (
        contract(table_real, real_part) - contract(table_imag, imag_part),
        contract(table_real, imag_part) + contract(table_imag, real_part),
    )


def spectral_order(length):
    if length <= 256:
        return np.arange(length)
    outer_len = length // 128
    return (spectral_order(outer_len)[:, None] + outer_len * np.arange(128)[None, :]).reshape(-1)


def whole_forward(real_part, imag_part, length):
    if length <= 256:
        table_real, table_imag = dft_table(length, -1.0)
        return complex_apply("kn,...n->...k", table_real, table_imag, real_part, imag_part)
    inner_len = 128
    outer_len = length // inner_len
    lead = real_part.shape[:-1]
    real_part = jnp.swapaxes(real_part.reshape(lead + (outer_len, inner_len)), -1, -2)
    imag_part = jnp.swapaxes(imag_part.reshape(lead + (outer_len, inner_len)), -1, -2)
    real_part, imag_part = whole_forward(real_part, imag_part, outer_len)
    real_part = jnp.swapaxes(real_part, -1, -2)
    imag_part = jnp.swapaxes(imag_part, -1, -2)
    freq_idx = jnp.asarray(spectral_order(outer_len), dtype=jnp.int32)[:, None]
    inner_idx = jnp.arange(inner_len, dtype=jnp.int32)[None, :]
    cos_part, sin_part = twiddle(freq_idx * inner_idx, length)
    real_part, imag_part = rotate(real_part, imag_part, cos_part, -sin_part)
    table_real, table_imag = dft_table(inner_len, -1.0)
    real_part, imag_part = complex_apply(
        "ub,...tb->...tu", table_real, table_imag, real_part, imag_part
    )
    return (real_part.reshape(lead + (length,)), imag_part.reshape(lead + (length,)))


def whole_inverse(real_part, imag_part, length):
    if length <= 256:
        table_real, table_imag = dft_table(length, 1.0)
        return complex_apply("kn,...n->...k", table_real, table_imag, real_part, imag_part)
    inner_len = 128
    outer_len = length // inner_len
    lead = real_part.shape[:-1]
    real_part = real_part.reshape(lead + (outer_len, inner_len))
    imag_part = imag_part.reshape(lead + (outer_len, inner_len))
    table_real, table_imag = dft_table(inner_len, 1.0)
    real_part, imag_part = complex_apply(
        "bu,...tu->...tb", table_real, table_imag, real_part, imag_part
    )
    freq_idx = jnp.asarray(spectral_order(outer_len), dtype=jnp.int32)[:, None]
    inner_idx = jnp.arange(inner_len, dtype=jnp.int32)[None, :]
    cos_part, sin_part = twiddle(freq_idx * inner_idx, length)
    real_part, imag_part = rotate(real_part, imag_part, cos_part, sin_part)
    real_part, imag_part = whole_inverse(
        jnp.swapaxes(real_part, -1, -2), jnp.swapaxes(imag_part, -1, -2), outer_len
    )
    real_part = jnp.swapaxes(real_part, -1, -2)
    imag_part = jnp.swapaxes(imag_part, -1, -2)
    return (real_part.reshape(lead + (length,)), imag_part.reshape(lead + (length,)))


def owner_conv(stacked, groups, samples):
    chan_rows = stacked.shape[1]
    own_rows = chan_rows // groups
    span = groups * samples
    pieces = stacked.reshape(2, groups, own_rows, samples)
    rows_whole = lax.all_to_all(pieces, "seq", split_axis=1, concat_axis=3, tiled=True).reshape(
        2, own_rows, span
    )
    padded = jnp.concatenate([rows_whole, jnp.zeros_like(rows_whole)], axis=2)
    spec_real, spec_imag = whole_forward(padded, jnp.zeros_like(padded), 2 * span)
    prod_real = spec_real[0] * spec_real[1] - spec_imag[0] * spec_imag[1]
    prod_imag = spec_real[0] * spec_imag[1] + spec_imag[0] * spec_real[1]
    back_real, back_imag = whole_inverse(prod_real, prod_imag, 2 * span)
    conv_rows = back_real[:, :span]
    return lax.all_to_all(conv_rows, "seq", split_axis=1, concat_axis=0, tiled=True)


def per_device(signal, gating, response, skip_gain, mixing_weight):
    chan_rows, samples = signal.shape
    groups = lax.axis_size("seq")
    full_len = 2 * groups * samples
    stacked = jnp.stack([signal, response])
    conv = owner_conv(stacked, groups, samples)
    conv = conv / full_len
    mixed_in = gating * (conv + skip_gain[:, None] * signal)
    return lax.psum_scatter(
        jnp.dot(
            mixing_weight,
            mixed_in,
            precision=lax.Precision.HIGHEST,
            preferred_element_type=jnp.float32,
        ),
        "chan",
        scatter_dimension=0,
        tiled=True,
    )


def solution(mesh):
    in_specs = (P("chan", "seq"), P("chan", "seq"), P("chan", "seq"), P("chan"), P(None, "chan"))
    out_specs = P("chan", "seq")
    return jax.shard_map(
        per_device, mesh=mesh, in_specs=in_specs, out_specs=out_specs, check_vma=False
    )
```

profile of v0, /device:TPU:0, one launch (start us, length us, event | category | flops | bytes accessed | tf_op | source)
XLA Modules:
  0.0 486.4 jit_solution(6807660299492079792)
XLA Ops:
  6.5 4.6 pad_maximum_fusion
  11.1 7.4 %all-to-all-start = ((f32[2,8,8,8192]{3,2,0,1:T(8,128)}), f32[2,8,8,8192]{3,2,0,1:T(8,128)}, u32[]{:S(2)}, u32[]{:S(2)}) async-start(f32[2,8,8,8192]{3,2,0,1:T(8,128)} %pad_maximum_fusion), calls=%async_computation | async-start | bytes 8388608 | tf_op jit(solution)/shard_map/all_to_all | solution.py:96
  18.6 0.0 reduce-scatter.4.cloned.1.call-start
  18.6 0.1 sine_negate_fusion.1
  18.7 0.1 fusion.149
  18.7 2.1 fusion.70
  20.8 3.4 fusion.69
  24.3 8.9 %fusion.34 = f32[2,8,128,128,8]{3,4,2,1,0:T(8,128)} fusion(), kind=kOutput, calls=%fused_computation.58 | convolution fusion | flops 201327552 | bytes 8388608 | tf_op jit(solution)/shard_map/kn,...n->...k/dot_general | solution.py:31
  33.2 78.7 %all-to-all-done = f32[2,8,8,8192]{3,2,0,1:T(8,128)} async-done(((f32[2,8,8,8192]{3,2,0,1:T(8,128)}), f32[2,8,8,8192]{3,2,0,1:T(8,128)}, u32[]{:S(2)}, u32[]{:S(2)}) %all-to-all-start) | async-done | bytes 4194336 | tf_op jit(solution)/shard_map/all_to_all | solution.py:96
  111.8 6.6 %copy.47 = f32[2,1,8,8,8192]{4,3,2,0,1:T(8,128)} copy(f32[2,1,8,8,8192]{4,2,0,3,1:T(8,128)} %bitcast.3) | data formatting | bytes 8388608 | tf_op jit(solution)/shard_map/all_to_all | solution.py:96
  118.4 4.0 reshape.255
  122.4 2.7 pad_bitcast_fusion
  125.1 4.9 %copy.100 = f32[2,8,1024,128]{3,2,1,0:T(8,128)} copy(f32[2,8,1024,128]{3,1,2,0:T(8,128)S(1)} %pad_bitcast_fusion) | data formatting | bytes 16777216
  130.0 8.7 %copy.74 = f32[2,8,128,8,128]{4,3,2,1,0:T(8,128)} copy(f32[2,8,128,8,128]{2,4,3,1,0:T(8,128)} %bitcast.216) | data formatting | bytes 16777216 | tf_op jit(solution)/shard_map/reshape | solution.py:50
  138.6 12.5 %fusion.4 = f32[2,8,128,128,8]{3,4,2,1,0:T(8,128)} fusion(f32[2,8,128,8,128]{4,3,2,1,0:T(8,128)} %copy.74), kind=kOutput, calls=%fused_computation.14 | convolution fusion | flops 201327552 | bytes 16777216 | tf_op jit(solution)/shard_map/kn,...n->...k/dot_general | solution.py:32
  151.1 9.3 %fusion.6 = f32[2,8,128,128,8]{3,4,2,1,0:T(8,128)} fusion(f32[2,8,128,8,128]{4,3,2,1,0:T(8,128)S(1)} %copy-done.1), kind=kOutput, calls=%fused_computation.16 | convolution fusion | flops 201327488 | bytes 16777216 | tf_op jit(solution)/shard_map/kn,...n->...k/dot_general | solution.py:31
  160.4 15.3 %fusion.2 = (f32[2,8,128,8,128]{4,3,2,1,0:T(8,128)}, f32[2,8,128,8,128]{4,3,2,1,0:T(8,128)S(1)}) fusion(f32[8,128]{1,0:T(8,128)S(1)} %get-tuple-element.19, f32[8,128]{1,0:T(8,128)S(1)} %get-tuple-element.20, f32[2,8,128,128,8]{3,4,2,1,0:T(8,128)} %fusion.4, f32[2,8,128,128,8]{3,4,2,1,0:T(8,128)} %fusion.6, f32[2,8,128,128,8]{3,4,2,1,0:T(8,128)} %fusion.34), kind=kOutput, calls=%fused_computation.10 | convolution fusion | flops 218104704 | bytes 41951232 | tf_op jit(solution)/shard_map/kn,...n->...k/dot_general | solution.py:32
  175.7 11.1 %fusion.8 = f32[2,8,128,8,128]{2,4,3,1,0:T(8,128)} fusion(f32[2,8,128,8,128]{4,3,2,1,0:T(8,128)S(1)} %get-tuple-element.6), kind=kOutput, calls=%fused_computation.19 | convolution fusion | flops 3221454848 | bytes 16777216 | tf_op jit(solution)/shard_map/ub,...tb->...tu/dot_general | solution.py:32
  186.8 8.8 %fusion.10 = f32[2,8,128,8,128]{2,4,3,1,0:T(8,128)S(1)} fusion(f32[2,8,128,8,128]{4,3,2,1,0:T(8,128)S(1)} %get-tuple-element.6), kind=kOutput, calls=%fused_computation.21 | convolution fusion | flops 3221471232 | bytes 16777216 | tf_op jit(solution)/shard_map/ub,...tb->...tu/dot_general | solution.py:31
  195.7 13.0 %fusion.39 = f32[2,8,128,8,128]{2,4,3,1,0:T(8,128)} fusion(f32[2,8,128,8,128]{2,4,3,1,0:T(8,128)} %fusion.8, f32[2,8,128,8,128]{4,3,2,1,0:T(8,128)S(1)} %bitcast.211), kind=kOutput, calls=%fused_computation.61 | convolution fusion | flops 3223568384 | bytes 25165824 | tf_op jit(solution)/shard_map/ub,...tb->...tu/dot_general | solution.py:32
  208.7 10.7 %fusion.36 = f32[2,8,128,8,128]{2,4,3,1,0:T(8,128)} fusion(f32[2,8,128,8,128]{2,4,3,1,0:T(8,128)S(1)} %fusion.10, f32[2,8,128,8,128]{4,3,2,1,0:T(8,128)S(1)} %bitcast.211), kind=kOutput, calls=%fused_computation.60 | convolution fusion | flops 3223552000 | bytes 25165824 | tf_op jit(solution)/shard_map/ub,...tb->...tu/dot_general | solution.py:31
  219.4 7.0 %fusion = (f32[2,8,1024,128]{3,2,1,0:T(8,128)S(1)}, f32[2,8,1024,128]{3,2,1,0:T(8,128)S(1)}) fusion(f32[2,8,128,8,128]{2,4,3,1,0:T(8,128)} %fusion.36, f32[2,8,128,8,128]{2,4,3,1,0:T(8,128)} %fusion.39, f32[1024,128]{1,0:T(8,128)S(1)} %get-tuple-element.18, f32[1024,128]{1,0:T(8,128)S(1)} %get-tuple-element.17), kind=kLoop, calls=%fused_computation.4 | loop fusion | flops 12582912 | bytes 34603008 | tf_op jit(solution)/shard_map/sub | solution.py:17
  226.5 9.7 %fusion.88 = f32[2,8,1024,128]{3,2,1,0:T(8,128)} fusion(f32[2,8,1024,128]{3,2,1,0:T(8,128)S(1)} %get-tuple-element.7), kind=kOutput, calls=%fused_computation.116 | convolution fusion | flops 3221454848 | bytes 16777216 | tf_op jit(solution)/shard_map/ub,...tb->...tu/dot_general | solution.py:31
  236.2 7.8 %fusion.86 = f32[2,8,1024,128]{3,2,1,0:T(8,128)S(1)} fusion(f32[2,8,1024,128]{3,2,1,0:T(8,128)S(1)} %get-tuple-element.8), kind=kOutput, calls=%fused_computation.114 | convolution fusion | flops 3221454848 | bytes 16777216 | tf_op jit(solution)/shard_map/ub,...tb->...tu/dot_general | solution.py:32
  244.0 11.4 %convolution_subtract_fusion = f32[2,8,1024,128]{3,2,1,0:T(8,128)} fusion(f32[2,8,1024,128]{3,2,1,0:T(8,128)} %fusion.88, f32[2,8,1024,128]{3,2,1,0:T(8,128)S(1)} %get-tuple-element.8), kind=kOutput, calls=%fused_computation.63 | convolution fusion | flops 3223568384 | bytes 25165824 | tf_op jit(solution)/shard_map/ub,...tb->...tu/dot_general | solution.py:31
  255.4 9.5 %convolution_add_fusion = f32[2,8,1024,128]{3,2,1,0:T(8,128)} fusion(f32[2,8,1024,128]{3,2,1,0:T(8,128)S(1)} %fusion.86, f32[2,8,1024,128]{3,2,1,0:T(8,128)S(1)} %get-tuple-element.7), kind=kOutput, calls=%fused_computation.62 | convolution fusion | flops 3223568384 | bytes 25165824 | tf_op jit(solution)/shard_map/ub,...tb->...tu/dot_general | solution.py:32
  264.9 4.2 multiply_subtract_fusion
  269.1 3.8 fusion.22
  272.9 3.8 fusion.20
  276.8 0.0 copy-start.4
  276.8 3.8 fusion.44
  280.6 5.2 %fusion.18 = (f32[8,128,1024]{1,2,0:T(8,128)S(1)}, f32[8,128,1024]{1,2,0:T(8,128)S(1)}) fusion(f32[8,1024,128]{2,1,0:T(8,128)S(1)} %fusion.44, f32[128,1024]{0,1:T(8,128)S(1)} %copy-done.5, f32[128,1024]{0,1:T(8,128)S(1)} %copy-done.4, f32[8,1024,128]{2,1,0:T(8,128)S(1)} %fusion.20, f32[1,8,1024,128]{3,2,1,0:T(8,128)S(1)} %get-tuple-element.9), kind=kOutput, calls=%fused_computation.37 | convolution fusion | flops 1618182144 | bytes 22020096 | tf_op jit(solution)/shard_map/bu,...tu->...tb/dot_general | solution.py:32
  285.9 7.0 %fusion.84 = f32[8,128,8,128]{3,1,2,0:T(8,128)S(1)} fusion(f32[8,128,8,128]{1,3,2,0:T(8,128)S(1)} %bitcast.212), kind=kOutput, calls=%fused_computation.112 | convolution fusion | flops 1610842112 | bytes 8388608 | tf_op jit(solution)/shard_map/bu,...tu->...tb/dot_general | solution.py:31
  292.9 7.3 %fusion.82 = f32[8,128,8,128]{3,1,2,0:T(8,128)S(1)} fusion(f32[8,128,8,128]{1,3,2,0:T(8,128)S(1)} %bitcast.214), kind=kOutput, calls=%fused_computation.110 | convolution fusion | flops 1610842112 | bytes 8388608 | tf_op jit(solution)/shard_map/bu,...tu->...tb/dot_general | solution.py:32
  300.2 7.1 %convolution_subtract_fusion.1 = f32[8,128,8,128]{3,1,2,0:T(8,128)S(1)} fusion(f32[8,128,8,128]{3,1,2,0:T(8,128)S(1)} %fusion.84, f32[8,128,8,128]{1,3,2,0:T(8,128)S(1)} %bitcast.215), kind=kOutput, calls=%fused_computation.67 | convolution fusion | flops 1611890688 | bytes 12582912 | tf_op jit(solution)/shard_map/bu,...tu->...tb/dot_general | solution.py:31
  307.3 7.3 %fusion.16 = (f32[8,128,128,8]{2,1,3,0:T(8,128)S(1)}, f32[8,128,128,8]{2,1,3,0:T(8,128)S(1)}) fusion(f32[8,128,8,128]{3,1,2,0:T(8,128)S(1)} %convolution_subtract_fusion.1, f32[128,8]{0,1:T(8,128)S(1)} %get-tuple-element.21, f32[128,8]{0,1:T(8,128)S(1)} %get-tuple-element.22, f32[8,128,8,128]{3,1,2,0:T(8,128)S(1)} %fusion.82, ...), kind=kOutput, calls=%fused_computation.31 | convolution fusion | flops 1618182144 | bytes 20979712 | tf_op jit(solution)/shard_map/bu,...tu->...tb/dot_general | solution.py:32
  314.6 6.6 %fusion.28 = f32[8,128,128,8]{2,3,1,0:T(8,128)S(1)} fusion(f32[8,128,128,8]{2,1,3,0:T(8,128)S(1)} %get-tuple-element.14), kind=kOutput, calls=%fused_computation.49 | convolution fusion | flops 100664192 | bytes 8388608 | tf_op jit(solution)/shard_map/kn,...n->...k/dot_general | solution.py:31
  321.2 6.9 %subtract_bitcast_fusion = f32[8,128,8,128]{3,2,1,0:T(8,128)} fusion(f32[8,128,128,8]{2,3,1,0:T(8,128)S(1)} %fusion.28, f32[8,128,128,8]{2,1,3,0:T(8,128)S(1)} %get-tuple-element.13), kind=kOutput, calls=%fused_computation.53 | convolution fusion | flops 101712768 | bytes 12582912 | tf_op jit(solution)/shard_map/kn,...n->...k/dot_general | solution.py:31
  328.1 5.4 %copy.75 = f32[8,128,8,128]{1,3,2,0:T(8,128)} copy(f32[8,128,8,128]{3,2,1,0:T(8,128)} %subtract_bitcast_fusion) | data formatting | bytes 8388608 | tf_op jit(solution)/shard_map/reshape | solution.py:88
  333.5 4.6 copy.101
  338.1 0.0 copy-start.3
  338.1 0.0 copy-start.8
  338.1 0.1 slice.32
  338.3 52.3 %all_to_all.28 = f32[8,8,8192]{2,0,1:T(8,128)S(1)} all-to-all(f32[8,8,8192]{2,0,1:T(8,128)S(1)} %bitcast.219), channel_id=1, replica_groups=mesh['seq'=8,'chan'=4] {'seq'}, dimensions={1} | all-to-all | bytes 4194304 | tf_op jit(solution)/shard_map/all_to_all | solution.py:105
  390.6 9.1 %convolution_bitcast_fusion = f32[256,8192]{0,1:T(8,128)} fusion(f32[256,64]{0,1:T(8,128)S(1)} %copy-done, f32[64,8192]{1,0:T(8,128)S(1)} %copy-done.6, f32[64,8192]{1,0:T(8,128)S(1)} %copy-done.3, f32[8,8,8192]{2,0,1:T(8,128)S(1)} %all_to_all.28, f32[64]{0:T(128)S(1)} %copy-done.8), kind=kOutput, calls=%fused_computation | convolution fusion | flops 1612709888 | bytes 14745856 | tf_op jit(solution)/shard_map/dot_general | solution.py:117
  399.7 8.9 %copy.76 = f32[256,8192]{1,0:T(8,128)} copy(f32[256,8192]{0,1:T(8,128)} %convolution_bitcast_fusion) | data formatting | bytes 16777216
  408.6 0.0 reduce-scatter.4.cloned.1.call-update
  408.6 70.6 %reduce-scatter.4.cloned.1.call-done = f32[64,8192]{1,0:T(8,128)} async-done(((f32[256,8192]{1,0:T(8,128)}), f32[64,8192]{1,0:T(8,128)}) %reduce-scatter.4.cloned.1.call-update) | async-done | bytes 2097168 | tf_op jit(solution)/shard_map/reduce_scatter | solution.py:116
  (20 shorter events, 0.0 us)
Async XLA Ops:
  6.5 384.1 %copy-start = (f32[256,64]{0,1:T(8,128)S(1)}, f32[256,64]{0,1:T(8,128)}, u32[]{:S(2)}) copy-start(f32[256,64]{0,1:T(8,128)} %param.13) | copy-start | bytes 196612
  11.1 7.6 %copy-start.7 = (s32[1024]{0:T(1024)S(1)}, s32[1024]{0:T(1024)}, u32[]{:S(2)}) copy-start(s32[1024]{0:T(1024)} %constant.100.clone) | copy-start | bytes 12292
  11.1 100.7 %all-to-all-start = ((f32[2,8,8,8192]{3,2,0,1:T(8,128)}), f32[2,8,8,8192]{3,2,0,1:T(8,128)}, u32[]{:S(2)}, u32[]{:S(2)}) async-start(f32[2,8,8,8192]{3,2,0,1:T(8,128)} %pad_maximum_fusion), calls=%async_computation | async-start | bytes 8388608 | tf_op jit(solution)/shard_map/all_to_all | solution.py:96
  18.6 460.7 %reduce-scatter.4.cloned.1.call-start = ((), (), s32[]{:S(2)}) async-start(), calls=%async_computation.3 | async-start | bytes 10485760 | tf_op jit(solution)/shard_map/reduce_scatter | solution.py:116
  138.6 12.5 %copy-start.1 = (f32[2,8,128,8,128]{4,3,2,1,0:T(8,128)S(1)}, f32[2,8,128,8,128]{4,3,2,1,0:T(8,128)}, u32[]{:S(2)}) copy-start(f32[2,8,128,8,128]{4,3,2,1,0:T(8,128)} %copy.74) | copy-start | bytes 25165828
  175.7 20.0 %slice-start = ((s8[8388608]{0:T(1024)(128)(4,1)}), s8[4194304]{0:T(1024)(128)(4,1)S(1)}, s32[]{:S(2)}) async-start(s8[8388608]{0:T(1024)(128)(4,1)} %bitcast.210), calls=%async_computation.4 | async-start | bytes 8388608
  186.8 8.9 %slice-start.1 = ((s8[8388608]{0:T(1024)(128)(4,1)}), s8[4194304]{0:T(1024)(128)(4,1)S(1)}, s32[]{:S(2)}) async-start(s8[8388608]{0:T(1024)(128)(4,1)} %bitcast.210), calls=%async_computation.5 | async-start | bytes 8388608
  255.4 9.5 %copy-start.2 = (f32[2,8,1024,128]{3,2,1,0:T(8,128)S(1)}, f32[2,8,1024,128]{3,2,1,0:T(8,128)}, u32[]{:S(2)}) copy-start(f32[2,8,1024,128]{3,2,1,0:T(8,128)} %convolution_subtract_fusion) | copy-start | bytes 25165828
  276.8 3.9 copy-start.4
  276.8 3.9 copy-start.5
  338.1 52.5 %copy-start.3 = (f32[64,8192]{1,0:T(8,128)S(1)}, f32[64,8192]{1,0:T(8,128)}, u32[]{:S(2)}) copy-start(f32[64,8192]{1,0:T(8,128)} %param.9) | copy-start | bytes 6291460
  338.1 52.5 %copy-start.6 = (f32[64,8192]{1,0:T(8,128)S(1)}, f32[64,8192]{1,0:T(8,128)}, u32[]{:S(2)}) copy-start(f32[64,8192]{1,0:T(8,128)} %param.10) | copy-start | bytes 6291460
  338.1 52.5 %copy-start.8 = (f32[64]{0:T(128)S(1)}, f32[64]{0:T(128)}, u32[]{:S(2)}) copy-start(f32[64]{0:T(128)} %param.12) | copy-start | bytes 772
Sparse Core Ops, SparseCore 0:
  408.8 70.4 reduce-scatter.3
where the time goes:
time: 490 us; the launch traced here: 486 us
  matrix products  196 us (40%)
  waiting for transfers between devices  149 us (30%)
  blocking collectives  52.3 us (11%)
  local copies, waits for them, and re-layouts  45.9 us (9%)
  other arithmetic  21.5 us (4%)
  between operations  13.9 us (3%)
  starting transfers between devices  7.45 us (2%)
    all_to_all x1, waiting for transfers between devices, owner_conv(): lax.all_to_all(pieces, 'seq', split_axis=1, concat_axis=3, tiled=True)  78.7 us
    reduce_scatter x1, waiting for transfers between devices, per_device(): lax.psum_scatter(jnp.dot(mixing_weight, mixed_in, precision=lax.Precision...  70.6 us
    all_to_all x1, blocking collectives, owner_conv(): lax.all_to_all(conv_rows, 'seq', split_axis=1, concat_axis=0, tiled=True)  52.3 us
    dot_general x5, matrix products, complex_apply(): contract(table_imag, real_part)  47.6 us
    dot_general x6, matrix products, complex_apply(): contract(table_real, real_part) - contract(table_imag, imag_part)  47.5 us
    dot_general x6, matrix products, complex_apply(): contract(table_imag, imag_part)  46.6 us
    dot_general x5, matrix products, complex_apply(): contract(table_real, imag_part) + contract(table_imag, real_part)  45.3 us
    unnamed x26, local copies, waits for them, and re-layouts  21.2 us
  transfers between devices with their start and end apart: 2, of which 2 were waited for; matrix products, arithmetic and copies ran while one was open for 3% of the time, Pallas kernels for 0%

commit v1 on v0

--- a/solution.py
+++ b/solution.py
@@ -5,6 +5,28 @@
 import numpy as np
 from jax import lax
 from jax.sharding import PartitionSpec as P
+
+
+def in_blocks(shard, dim, count):
+    before, after = (shard.shape[:dim], shard.shape[dim + 1 :])
+    return jnp.moveaxis(shard.reshape(*before, count, -1, *after), dim, 0)
+
+
+def laid_out(parts, dim):
+    dims = list(parts.shape[1:])
+    dims[dim] *= parts.shape[0]
+    return jnp.moveaxis(parts, 0, dim).reshape(dims)
+
+
+def sent_to_each(x, axis, split_dim, concat_dim):
+    devices, index = (lax.axis_size(axis), lax.axis_index(axis))
+    blocks = in_blocks(x, split_dim, devices)
+    outs = [blocks[index]]
+    for step in range(1, devices):
+        sent = blocks[(index + step) % devices]
+        outs.append(lax.ppermute(sent, axis, [(i, (i + step) % devices) for i in range(devices)]))
+    blocks = jnp.stack(outs)[(index - jnp.arange(devices)) % devices]
+    return laid_out(blocks, concat_dim)
 
 
 def twiddle(number, period):
@@ -93,9 +115,7 @@
     own_rows = chan_rows // groups
     span = groups * samples
     pieces = stacked.reshape(2, groups, own_rows, samples)
-    rows_whole = lax.all_to_all(pieces, "seq", split_axis=1, concat_axis=3, tiled=True).reshape(
-        2, own_rows, span
-    )
+    rows_whole = sent_to_each(pieces, "seq", 1, 3).reshape(2, own_rows, span)
     padded = jnp.concatenate([rows_whole, jnp.zeros_like(rows_whole)], axis=2)
     spec_real, spec_imag = whole_forward(padded, jnp.zeros_like(padded), 2 * span)
     prod_real = spec_real[0] * spec_real[1] - spec_imag[0] * spec_imag[1]

time: 490 us -> 500 us (1.020); the launches traced: 486 us -> 491 us
  waiting for transfers between devices: 149 us -> 101 us
  blocking collectives: 52.3 us -> 80.3 us
  local copies, waits for them, and re-layouts: 45.9 us -> 62.3 us
  starting transfers between devices: 7.45 us -> 13.7 us
    all_to_all x1 -> x0, waiting for transfers between devices: 78.7 us -> none  [owner_conv(): lax.all_to_all(pieces, 'seq', split_axis=1, concat_axis=3, tiled=True)]
    ppermute x0 -> x7, waiting for transfers between devices: none -> 30.6 us  [sent_to_each(): lax.ppermute(sent, axis, [(i, (i + step) % devices) for i in range(device...]
    all_to_all x1, blocking collectives: 52.3 us -> 80.3 us  [owner_conv(): lax.all_to_all(conv_rows, 'seq', split_axis=1, concat_axis=0, tiled=True)]
    ppermute x0 -> x7, starting transfers between devices: none -> 13.7 us  [sent_to_each(): lax.ppermute(sent, axis, [(i, (i + step) % devices) for i in range(device...]
    unnamed x26 -> x36, local copies, waits for them, and re-layouts: 21.2 us -> 31.5 us
    all_to_all x1 -> x0, starting transfers between devices: 7.41 us -> none  [owner_conv(): lax.all_to_all(pieces, 'seq', split_axis=1, concat_axis=3, tiled=True)]
    transpose x0 -> x1, local copies, waits for them, and re-layouts: none -> 6.62 us  [laid_out(): return jnp.moveaxis(parts, 0, dim).reshape(dims)]
    all_to_all x1 -> x0, local copies, waits for them, and re-layouts: 6.56 us -> none  [owner_conv(): lax.all_to_all(pieces, 'seq', split_axis=1, concat_axis=3, tiled=True)]
  transfers between devices with their start and end apart: 2 -> 8, of which waited for: 2 -> 3; matrix products, arithmetic and copies ran while one was open for 3% -> 6% of each run, Pallas kernels for 0% -> 0%
where the time goes in v1:
time: 500 us; the launch traced here: 491 us
  matrix products  196 us (39%)
  waiting for transfers between devices  101 us (20%)
  blocking collectives  80.3 us (16%)
  local copies, waits for them, and re-layouts  62.3 us (12%)
  other arithmetic  23.3 us (5%)
  between operations  14.1 us (3%)
  starting transfers between devices  13.7 us (3%)
    all_to_all x1, blocking collectives, owner_conv(): lax.all_to_all(conv_rows, 'seq', split_axis=1, concat_axis=0, tiled=True)  80.3 us
    reduce_scatter x1, waiting for transfers between devices, per_device(): lax.psum_scatter(jnp.dot(mixing_weight, mixed_in, precision=lax.Precision...  70.5 us
    dot_general x6, matrix products, complex_apply(): contract(table_real, real_part) - contract(table_imag, imag_part)  47.6 us
    dot_general x5, matrix products, complex_apply(): contract(table_imag, real_part)  47.4 us
    dot_general x6, matrix products, complex_apply(): contract(table_imag, imag_part)  46.7 us
    dot_general x5, matrix products, complex_apply(): contract(table_real, imag_part) + contract(table_imag, real_part)  45.2 us
    unnamed x36, local copies, waits for them, and re-layouts  31.5 us
    ppermute x7, waiting for transfers between devices, sent_to_each(): lax.ppermute(sent, axis, [(i, (i + step) % devices) for i in range(device...  30.6 us
  transfers between devices with their start and end apart: 8, of which 3 were waited for; matrix products, arithmetic and copies ran while one was open for 6% of the time, Pallas kernels for 0%

profile of v1, /device:TPU:0, one launch (start us, length us, event | category | flops | bytes accessed | tf_op | source)
XLA Modules:
  0.0 490.7 jit_solution(15497374753521021417)
XLA Ops:
  6.5 3.7 fusion.63
  10.2 3.0 collective-permute-start
  14.8 2.6 collective-permute-start.2
  18.6 2.6 collective-permute-start.4
  24.2 2.1 fusion.87
  26.3 3.3 fusion.86
  29.6 8.9 %fusion.34 = f32[2,8,128,128,8]{3,4,2,1,0:T(8,128)} fusion(), kind=kOutput, calls=%fused_computation.74 | convolution fusion | flops 201327552 | bytes 8388608 | tf_op jit(solution)/shard_map/kn,...n->...k/dot_general | solution.py:53
  39.9 1.9 bitcast_dynamic-update-slice_fusion.6
  45.1 28.5 %collective-permute-done.2 = f32[2,1,8,8192]{3,2,0,1:T(8,128)} collective-permute-done((f32[2,1,8,8192]{3,2,0,1:T(8,128)}, f32[2,1,8,8192]{3,2,0,1:T(8,128)}, u32[]{:S(2)}, u32[]{:S(2)}) %collective-permute-start.2) | collective-permute-done | bytes 524320 | tf_op jit(solution)/shard_map/ppermute | solution.py:27
  73.6 1.9 bitcast_dynamic-update-slice_fusion.4
  75.5 1.9 bitcast_dynamic-update-slice_fusion.3
  77.4 1.9 bitcast_dynamic-update-slice_fusion.2
  80.1 2.0 collective-permute-done.6
  83.0 4.9 %gather_fusion = f32[8,2,8,8192]{3,2,1,0:T(8,128)} fusion(f32[8,2,8,8192]{3,2,1,0:T(8,128)} %bitcast.19, s32[1024]{0:T(1024)S(1)} %pad_clamp_fusion), kind=kCustom, calls=%fused_computation | custom fusion | bytes 8388640 | tf_op jit(solution)/shard_map/gather | solution.py:28
  87.9 6.6 %copy.52 = f32[2,1,8,8,8192]{4,3,2,0,1:T(8,128)} copy(f32[2,1,8,8,8192]{4,2,0,3,1:T(8,128)} %bitcast.262) | data formatting | bytes 8388608 | tf_op jit(solution)/shard_map/transpose | solution.py:18
  94.6 4.1 reshape_reshape.4
  98.7 2.7 pad_bitcast_fusion
  101.4 4.9 copy.105
  106.3 8.7 %copy.79 = f32[2,8,128,8,128]{4,3,2,1,0:T(8,128)} copy(f32[2,8,128,8,128]{2,4,3,1,0:T(8,128)} %bitcast.258) | data formatting | bytes 16777216 | tf_op jit(solution)/shard_map/reshape | solution.py:72
  115.0 12.3 %fusion.4 = f32[2,8,128,128,8]{3,4,2,1,0:T(8,128)} fusion(f32[2,8,128,8,128]{4,3,2,1,0:T(8,128)} %copy.79), kind=kOutput, calls=%fused_computation.31 | convolution fusion | flops 201327552 | bytes 16777216 | tf_op jit(solution)/shard_map/kn,...n->...k/dot_general | solution.py:54
  127.2 9.3 %fusion.6 = f32[2,8,128,128,8]{3,4,2,1,0:T(8,128)} fusion(f32[2,8,128,8,128]{4,3,2,1,0:T(8,128)S(1)} %copy-done.1), kind=kOutput, calls=%fused_computation.33 | convolution fusion | flops 201327488 | bytes 16777216 | tf_op jit(solution)/shard_map/kn,...n->...k/dot_general | solution.py:53
  136.5 15.5 %fusion.2 = (f32[2,8,128,8,128]{4,3,2,1,0:T(8,128)}, f32[2,8,128,8,128]{4,3,2,1,0:T(8,128)S(1)}) fusion(f32[8,128]{1,0:T(8,128)S(1)} %get-tuple-element.25, f32[8,128]{1,0:T(8,128)S(1)} %get-tuple-element.26, f32[2,8,128,128,8]{3,4,2,1,0:T(8,128)} %fusion.4, f32[2,8,128,128,8]{3,4,2,1,0:T(8,128)} %fusion.6, f32[2,8,128,128,8]{3,4,2,1,0:T(8,128)} %fusion.34), kind=kOutput, calls=%fused_computation.27 | convolution fusion | flops 218104704 | bytes 41951232 | tf_op jit(solution)/shard_map/kn,...n->...k/dot_general | solution.py:54
  152.0 10.8 %fusion.8 = f32[2,8,128,8,128]{2,4,3,1,0:T(8,128)} fusion(f32[2,8,128,8,128]{4,3,2,1,0:T(8,128)S(1)} %get-tuple-element.6), kind=kOutput, calls=%fused_computation.36 | convolution fusion | flops 3221454848 | bytes 16777216 | tf_op jit(solution)/shard_map/ub,...tb->...tu/dot_general | solution.py:54
  162.8 8.8 %fusion.10 = f32[2,8,128,8,128]{2,4,3,1,0:T(8,128)S(1)} fusion(f32[2,8,128,8,128]{4,3,2,1,0:T(8,128)S(1)} %get-tuple-element.6), kind=kOutput, calls=%fused_computation.38 | convolution fusion | flops 3221471232 | bytes 16777216 | tf_op jit(solution)/shard_map/ub,...tb->...tu/dot_general | solution.py:53
  171.7 13.1 %fusion.39 = f32[2,8,128,8,128]{2,4,3,1,0:T(8,128)} fusion(f32[2,8,128,8,128]{2,4,3,1,0:T(8,128)} %fusion.8, f32[2,8,128,8,128]{4,3,2,1,0:T(8,128)S(1)} %bitcast.250), kind=kOutput, calls=%fused_computation.77 | convolution fusion | flops 3223568384 | bytes 25165824 | tf_op jit(solution)/shard_map/ub,...tb->...tu/dot_general | solution.py:54
  184.8 10.7 %fusion.36 = f32[2,8,128,8,128]{2,4,3,1,0:T(8,128)} fusion(f32[2,8,128,8,128]{2,4,3,1,0:T(8,128)S(1)} %fusion.10, f32[2,8,128,8,128]{4,3,2,1,0:T(8,128)S(1)} %bitcast.250), kind=kOutput, calls=%fused_computation.76 | convolution fusion | flops 3223552000 | bytes 25165824 | tf_op jit(solution)/shard_map/ub,...tb->...tu/dot_general | solution.py:53
  195.5 7.0 %fusion = (f32[2,8,1024,128]{3,2,1,0:T(8,128)S(1)}, f32[2,8,1024,128]{3,2,1,0:T(8,128)S(1)}) fusion(f32[2,8,128,8,128]{2,4,3,1,0:T(8,128)} %fusion.36, f32[2,8,128,8,128]{2,4,3,1,0:T(8,128)} %fusion.39, f32[1024,128]{1,0:T(8,128)S(1)} %get-tuple-element.24, f32[1024,128]{1,0:T(8,128)S(1)} %get-tuple-element.23), kind=kLoop, calls=%fused_computation.21 | loop fusion | flops 12582912 | bytes 34603008 | tf_op jit(solution)/shard_map/sub | solution.py:39
  202.6 9.8 %fusion.105 = f32[2,8,1024,128]{3,2,1,0:T(8,128)} fusion(f32[2,8,1024,128]{3,2,1,0:T(8,128)S(1)} %get-tuple-element.7), kind=kOutput, calls=%fused_computation.156 | convolution fusion | flops 3221454848 | bytes 16777216 | tf_op jit(solution)/shard_map/ub,...tb->...tu/dot_general | solution.py:53
  212.4 7.8 %fusion.103 = f32[2,8,1024,128]{3,2,1,0:T(8,128)S(1)} fusion(f32[2,8,1024,128]{3,2,1,0:T(8,128)S(1)} %get-tuple-element.8), kind=kOutput, calls=%fused_computation.154 | convolution fusion | flops 3221454848 | bytes 16777216 | tf_op jit(solution)/shard_map/ub,...tb->...tu/dot_general | solution.py:54
  220.1 11.5 %convolution_subtract_fusion = f32[2,8,1024,128]{3,2,1,0:T(8,128)} fusion(f32[2,8,1024,128]{3,2,1,0:T(8,128)} %fusion.105, f32[2,8,1024,128]{3,2,1,0:T(8,128)S(1)} %get-tuple-element.8), kind=kOutput, calls=%fused_computation.79 | convolution fusion | flops 3223568384 | bytes 25165824 | tf_op jit(solution)/shard_map/ub,...tb->...tu/dot_general | solution.py:53
  231.6 9.6 %convolution_add_fusion = f32[2,8,1024,128]{3,2,1,0:T(8,128)} fusion(f32[2,8,1024,128]{3,2,1,0:T(8,128)S(1)} %fusion.103, f32[2,8,1024,128]{3,2,1,0:T(8,128)S(1)} %get-tuple-element.7), kind=kOutput, calls=%fused_computation.78 | convolution fusion | flops 3223568384 | bytes 25165824 | tf_op jit(solution)/shard_map/ub,...tb->...tu/dot_general | solution.py:54
  241.2 4.2 multiply_subtract_fusion
  245.3 3.8 fusion.22
  249.2 3.8 fusion.20
  253.0 3.8 fusion.44
  256.9 5.2 %fusion.18 = (f32[8,128,1024]{1,2,0:T(8,128)S(1)}, f32[8,128,1024]{1,2,0:T(8,128)S(1)}) fusion(f32[8,1024,128]{2,1,0:T(8,128)S(1)} %fusion.44, f32[128,1024]{0,1:T(8,128)S(1)} %copy-done.6, f32[128,1024]{0,1:T(8,128)S(1)} %copy-done.5, f32[8,1024,128]{2,1,0:T(8,128)S(1)} %fusion.20, f32[1,8,1024,128]{3,2,1,0:T(8,128)S(1)} %get-tuple-element.9), kind=kOutput, calls=%fused_computation.53 | convolution fusion | flops 1618182144 | bytes 22020096 | tf_op jit(solution)/shard_map/bu,...tu->...tb/dot_general | solution.py:54
  262.1 7.0 %fusion.101 = f32[8,128,8,128]{3,1,2,0:T(8,128)S(1)} fusion(f32[8,128,8,128]{1,3,2,0:T(8,128)S(1)} %bitcast.251), kind=kOutput, calls=%fused_computation.152 | convolution fusion | flops 1610842112 | bytes 8388608 | tf_op jit(solution)/shard_map/bu,...tu->...tb/dot_general | solution.py:53
  269.2 7.3 %fusion.99 = f32[8,128,8,128]{3,1,2,0:T(8,128)S(1)} fusion(f32[8,128,8,128]{1,3,2,0:T(8,128)S(1)} %bitcast.253), kind=kOutput, calls=%fused_computation.150 | convolution fusion | flops 1610842112 | bytes 8388608 | tf_op jit(solution)/shard_map/bu,...tu->...tb/dot_general | solution.py:54
  276.4 7.1 %convolution_subtract_fusion.1 = f32[8,128,8,128]{3,1,2,0:T(8,128)S(1)} fusion(f32[8,128,8,128]{3,1,2,0:T(8,128)S(1)} %fusion.101, f32[8,128,8,128]{1,3,2,0:T(8,128)S(1)} %bitcast.254), kind=kOutput, calls=%fused_computation.83 | convolution fusion | flops 1611890688 | bytes 12582912 | tf_op jit(solution)/shard_map/bu,...tu->...tb/dot_general | solution.py:53
  283.5 7.3 %fusion.16 = (f32[8,128,128,8]{2,1,3,0:T(8,128)S(1)}, f32[8,128,128,8]{2,1,3,0:T(8,128)S(1)}) fusion(f32[8,128,8,128]{3,1,2,0:T(8,128)S(1)} %convolution_subtract_fusion.1, f32[128,8]{0,1:T(8,128)S(1)} %get-tuple-element.27, f32[128,8]{0,1:T(8,128)S(1)} %get-tuple-element.28, f32[8,128,8,128]{3,1,2,0:T(8,128)S(1)} %fusion.99, ...), kind=kOutput, calls=%fused_computation.47 | convolution fusion | flops 1618182144 | bytes 20979712 | tf_op jit(solution)/shard_map/bu,...tu->...tb/dot_general | solution.py:54
  290.8 6.6 %fusion.28 = f32[8,128,128,8]{2,3,1,0:T(8,128)S(1)} fusion(f32[8,128,128,8]{2,1,3,0:T(8,128)S(1)} %get-tuple-element.14), kind=kOutput, calls=%fused_computation.65 | convolution fusion | flops 100664192 | bytes 8388608 | tf_op jit(solution)/shard_map/kn,...n->...k/dot_general | solution.py:53
  297.4 6.9 %subtract_bitcast_fusion = f32[8,128,8,128]{3,2,1,0:T(8,128)} fusion(f32[8,128,128,8]{2,3,1,0:T(8,128)S(1)} %fusion.28, f32[8,128,128,8]{2,1,3,0:T(8,128)S(1)} %get-tuple-element.13), kind=kOutput, calls=%fused_computation.69 | convolution fusion | flops 101712768 | bytes 12582912 | tf_op jit(solution)/shard_map/kn,...n->...k/dot_general | solution.py:53
  304.3 5.4 %copy.80 = f32[8,128,8,128]{1,3,2,0:T(8,128)} copy(f32[8,128,8,128]{3,2,1,0:T(8,128)} %subtract_bitcast_fusion) | data formatting | bytes 8388608 | tf_op jit(solution)/shard_map/reshape | solution.py:110
  309.7 4.6 copy.106
  314.5 80.3 %all_to_all.13 = f32[8,8,8192]{2,0,1:T(8,128)S(1)} all-to-all(f32[8,8,8192]{2,0,1:T(8,128)S(1)} %bitcast.265), channel_id=1, replica_groups=mesh['seq'=8,'chan'=4] {'seq'}, dimensions={1} | all-to-all | bytes 4194304 | tf_op jit(solution)/shard_map/all_to_all | solution.py:125
  394.8 9.1 %convolution_bitcast_fusion = f32[256,8192]{0,1:T(8,128)} fusion(f32[256,64]{0,1:T(8,128)S(1)} %copy-done, f32[64,8192]{1,0:T(8,128)S(1)} %copy-done.7, f32[64,8192]{1,0:T(8,128)S(1)} %copy-done.4, f32[8,8,8192]{2,0,1:T(8,128)S(1)} %all_to_all.13, f32[64]{0:T(128)S(1)} %copy-done.10), kind=kOutput, calls=%fused_computation.1 | convolution fusion | flops 1612709888 | bytes 14745856 | tf_op jit(solution)/shard_map/dot_general | solution.py:137
  403.9 9.0 %copy.81 = f32[256,8192]{1,0:T(8,128)} copy(f32[256,8192]{0,1:T(8,128)} %convolution_bitcast_fusion) | data formatting | bytes 16777216
  412.9 70.5 %reduce-scatter.4.cloned.1.call-done = f32[64,8192]{1,0:T(8,128)} async-done(((f32[256,8192]{1,0:T(8,128)}), f32[64,8192]{1,0:T(8,128)}) %reduce-scatter.4.cloned.1.call-update) | async-done | bytes 2097168 | tf_op jit(solution)/shard_map/reduce_scatter | solution.py:136
  (48 shorter events, 12.4 us)
Async XLA Ops:
  6.5 388.3 %copy-start = (f32[256,64]{0,1:T(8,128)S(1)}, f32[256,64]{0,1:T(8,128)}, u32[]{:S(2)}) copy-start(f32[256,64]{0,1:T(8,128)} %param.13) | copy-start | bytes 196612
  6.5 14.8 %copy-start.3 = (f32[64,8192]{1,0:T(8,128)S(1)}, f32[64,8192]{1,0:T(8,128)}, u32[]{:S(2)}) copy-start(f32[64,8192]{1,0:T(8,128)} %param.9) | copy-start | bytes 6291460
  6.5 476.9 %reduce-scatter.4.cloned.1.call-start = ((), (), s32[]{:S(2)}) async-start(), calls=%async_computation.2 | async-start | bytes 10485760 | tf_op jit(solution)/shard_map/reduce_scatter | solution.py:136
  10.2 28.3 %collective-permute-start = (f32[2,1,8,8192]{3,2,0,1:T(8,128)}, f32[2,1,8,8192]{3,2,0,1:T(8,128)}, u32[]{:S(2)}, u32[]{:S(2)}) collective-permute-start(f32[2,1,8,8192]{3,2,0,1:T(8,128)} %get-tuple-element.16), channel_id=1, source_target_pairs={{0,4},{4,8},{8,12},{12,16},{16,20},{20,24},{24,28},{28,0},{1,5},{5... | collective-permute-start | bytes 1572872 | tf_op jit(solution)/shard_map/ppermute | solution.py:27
  13.2 28.6 %collective-permute-start.1 = (f32[2,1,8,8192]{3,2,0,1:T(8,128)}, f32[2,1,8,8192]{3,2,0,1:T(8,128)}, u32[]{:S(2)}, u32[]{:S(2)}) collective-permute-start(f32[2,1,8,8192]{3,2,0,1:T(8,128)} %get-tuple-element.17), channel_id=1, source_target_pairs={{0,8},{4,12},{8,16},{12,20},{16,24},{20,28},{24,0},{28,4},{1,9},{5... | collective-permute-start | bytes 1572872 | tf_op jit(solution)/shard_map/ppermute | solution.py:27
  14.8 58.8 %collective-permute-start.2 = (f32[2,1,8,8192]{3,2,0,1:T(8,128)}, f32[2,1,8,8192]{3,2,0,1:T(8,128)}, u32[]{:S(2)}, u32[]{:S(2)}) collective-permute-start(f32[2,1,8,8192]{3,2,0,1:T(8,128)} %get-tuple-element.18), channel_id=1, source_target_pairs={{0,12},{4,16},{8,20},{12,24},{16,28},{20,0},{24,4},{28,8},{1,13},{... | collective-permute-start | bytes 1572872 | tf_op jit(solution)/shard_map/ppermute | solution.py:27
  17.3 58.1 %collective-permute-start.3 = (f32[2,1,8,8192]{3,2,0,1:T(8,128)}, f32[2,1,8,8192]{3,2,0,1:T(8,128)}, u32[]{:S(2)}, u32[]{:S(2)}) collective-permute-start(f32[2,1,8,8192]{3,2,0,1:T(8,128)} %get-tuple-element.19), channel_id=1, source_target_pairs={{0,16},{4,20},{8,24},{12,28},{16,0},{20,4},{24,8},{28,12},{1,17},{... | collective-permute-start | bytes 1572872 | tf_op jit(solution)/shard_map/ppermute | solution.py:27
  18.6 58.8 %collective-permute-start.4 = (f32[2,1,8,8192]{3,2,0,1:T(8,128)}, f32[2,1,8,8192]{3,2,0,1:T(8,128)}, u32[]{:S(2)}, u32[]{:S(2)}) collective-permute-start(f32[2,1,8,8192]{3,2,0,1:T(8,128)} %get-tuple-element.20), channel_id=1, source_target_pairs={{0,20},{4,24},{8,28},{12,0},{16,4},{20,8},{24,12},{28,16},{1,21},{... | collective-permute-start | bytes 1572872 | tf_op jit(solution)/shard_map/ppermute | solution.py:27
  21.3 2.9 copy-start.9
  29.6 12.2 %copy-start.8 = (f32[2,1,8,8192]{3,2,0,1:T(8,128)S(1)}, f32[2,1,8,8192]{3,2,0,1:T(8,128)}, u32[]{:S(2)}) copy-start(f32[2,1,8,8192]{3,2,0,1:T(8,128)} %get-tuple-element.15) | copy-start | bytes 1572868
  38.5 40.7 %collective-permute-start.5 = (f32[2,1,8,8192]{3,2,0,1:T(8,128)S(1)}, f32[2,1,8,8192]{3,2,0,1:T(8,128)S(1)}, u32[]{:S(2)}, u32[]{:S(2)}) collective-permute-start(f32[2,1,8,8192]{3,2,0,1:T(8,128)S(1)} %fusion.78), channel_id=1, source_target_pairs={{0,24},{4,28},{8,0},{12,4},{16,8},{20,12},{24,16},{28,20},{1,25},{... | collective-permute-start | bytes 1572872 | tf_op jit(solution)/shard_map/ppermute | solution.py:27
  41.8 40.4 %collective-permute-start.6 = (f32[2,1,8,8192]{3,2,0,1:T(8,128)S(1)}, f32[2,1,8,8192]{3,2,0,1:T(8,128)S(1)}, u32[]{:S(2)}, u32[]{:S(2)}) collective-permute-start(f32[2,1,8,8192]{3,2,0,1:T(8,128)S(1)} %copy-done.8), channel_id=1, source_target_pairs={{0,28},{4,0},{8,4},{12,8},{16,12},{20,16},{24,20},{28,24},{1,29},{... | collective-permute-start | bytes 1572872 | tf_op jit(solution)/shard_map/ppermute | solution.py:27
  115.0 12.3 %copy-start.1 = (f32[2,8,128,8,128]{4,3,2,1,0:T(8,128)S(1)}, f32[2,8,128,8,128]{4,3,2,1,0:T(8,128)}, u32[]{:S(2)}) copy-start(f32[2,8,128,8,128]{4,3,2,1,0:T(8,128)} %copy.79) | copy-start | bytes 25165828
  152.0 19.7 %slice-start = ((s8[8388608]{0:T(1024)(128)(4,1)}), s8[4194304]{0:T(1024)(128)(4,1)S(1)}, s32[]{:S(2)}) async-start(s8[8388608]{0:T(1024)(128)(4,1)} %bitcast.249), calls=%async_computation.3 | async-start | bytes 8388608
  162.8 8.9 %slice-start.1 = ((s8[8388608]{0:T(1024)(128)(4,1)}), s8[4194304]{0:T(1024)(128)(4,1)S(1)}, s32[]{:S(2)}) async-start(s8[8388608]{0:T(1024)(128)(4,1)} %bitcast.249), calls=%async_computation.4 | async-start | bytes 8388608
  231.6 9.6 %copy-start.2 = (f32[2,8,1024,128]{3,2,1,0:T(8,128)S(1)}, f32[2,8,1024,128]{3,2,1,0:T(8,128)}, u32[]{:S(2)}) copy-start(f32[2,8,1024,128]{3,2,1,0:T(8,128)} %convolution_subtract_fusion) | copy-start | bytes 25165828
  253.0 3.9 copy-start.5
  253.0 3.9 copy-start.6
  314.4 80.4 %copy-start.4 = (f32[64,8192]{1,0:T(8,128)S(1)}, f32[64,8192]{1,0:T(8,128)}, u32[]{:S(2)}) copy-start(f32[64,8192]{1,0:T(8,128)} %param.9) | copy-start | bytes 6291460
  314.4 80.4 %copy-start.7 = (f32[64,8192]{1,0:T(8,128)S(1)}, f32[64,8192]{1,0:T(8,128)}, u32[]{:S(2)}) copy-start(f32[64,8192]{1,0:T(8,128)} %param.10) | copy-start | bytes 6291460
  314.4 80.4 %copy-start.10 = (f32[64]{0:T(128)S(1)}, f32[64]{0:T(128)}, u32[]{:S(2)}) copy-start(f32[64]{0:T(128)} %param.12) | copy-start | bytes 772
Sparse Core Ops, SparseCore 0:
  413.1 70.3 reduce-scatter.3
